TPU v7x, 32 devices: a whole 2x2x4 slice. The times are simulated.
32 devices in a mesh: order: 1, shard: 32 (over z, y, x, core).
Axes of the slice: x: 2, y: 2, z: 4, core: 2. Of those that a mesh axis runs over, the one named last changes fastest.
Arguments:
- sky_coeffs: float32 [32, 2, 2048], P('shard'), may hold values from -6 to 6
- beam_coeffs: float32 [64, 2048], P('order'), may hold values from -0.09375 to 0.09375
- wigner: bfloat16 [32, 64, 2048, 128], P('shard', 'order'), may hold values from -0.125 to 0.125
- visits: int32 [32, 32, 4], P(('order', 'shard')), may hold values from -1 to 511, as said below
- point_slot: int32 [524288], P(('order', 'shard')), may hold values from 0 to 127, as said below
- phi_cell: int32 [524288], P(('order', 'shard')), may hold values from 0 to 30
- psi_cell: int32 [524288], P(('order', 'shard')), may hold values from 0 to 127
- fraction: float32 [2, 524288], P(None, ('order', 'shard')), may hold values from 0 to 1
Outputs:
- timeline: float32 [524288], P(('order', 'shard'))
Inputs may be any that keep to these rules, and one draw needn't show every extreme that they name: Live entries of one row visits[r, d] are distinct tiles of owner d and come first; every row holds 1 to 4 live entries; for every device r some owner d has all 4 entries live. `point_slot`: every pointing names a live entry of its own device's visit list. Of one device's pointings, exactly 768 name each of half of the owners and 256 each of the others.
All inputs are finite; a program needn't handle non-finite values.
Results may differ from a plain program's by a relative error of at most 0.008.
Values may be sent and summed in bfloat16 or wider, within the bound.
A program may use at most 128 MiB of HBM per device.

v0:
```python
import functools
import math

import jax
import jax.numpy as jnp
import numpy as np
from jax import lax
from jax.experimental import pallas as pl
from jax.experimental.pallas import tpu as pltpu
from jax.sharding import PartitionSpec as P

NPHI = 4096
NPSI = 128
PHI_T = 32
LOW = 8
LANES = 128
CHUNK = 256


SQUARE = 4
CORES = 2


def gather_blocks(lines, block_ref, out_ref, send_sem, recv_sem):
    me = lax.axis_index("shard")
    core = me % CORES
    square = me // CORES % SQUARE
    line = me // (CORES * SQUARE)
    depth = block_ref.shape[0]

    def index(at_line, at_square, at_core):
        return (at_line * SQUARE + at_square) * CORES + at_core

    along = [(line + d) % lines for d in range(1, lines)]
    if lines == 4:
        half = line // 2
        along = [line + 1 - 2 * (line % 2), 2 - half, 3 - 3 * half]
    across = [(square + d) % SQUARE for d in range(1, SQUARE)]
    other = (core + 1) % CORES
    line_peers = [index(a, square, core) for a in along]
    square_peers = [index(line, b, core) for b in across]
    twin = index(line, square, other)
    barrier = pltpu.get_barrier_semaphore()
    peers = line_peers + square_peers + [twin]
    for peer in peers:
        pl.semaphore_signal(
            barrier, inc=1, device_id={"shard": peer}, device_id_type=pl.DeviceIdType.MESH
        )
    pl.semaphore_wait(barrier, len(peers))

    started = []

    def place(owner):
        return out_ref.at[pl.ds(pl.multiple_of(owner * depth, depth), depth), :]

    def send(source, owner, peer):
        copy = pltpu.make_async_remote_copy(
            src_ref=source,
            dst_ref=place(owner),
            send_sem=send_sem.at[len(started)],
            recv_sem=recv_sem.at[owner],
            device_id={"shard": peer},
            device_id_type=pl.DeviceIdType.MESH,
        )
        copy.start()
        started.append(copy)

    def arrive(owner):
        pltpu.make_async_remote_copy(
            src_ref=place(owner),
            dst_ref=place(owner),
            send_sem=send_sem.at[0],
            recv_sem=recv_sem.at[owner],
            device_id={"shard": twin},
            device_id_type=pl.DeviceIdType.MESH,
        ).wait_recv()

    for peer in line_peers[::-1] + square_peers + [twin]:
        send(block_ref, me, peer)
    out_ref[pl.ds(pl.multiple_of(me * depth, depth), depth), :] = block_ref[...]
    for owner in line_peers:
        arrive(owner)
        for peer in square_peers + [twin]:
            send(place(owner), owner, peer)
    for a in [line] + along:
        for b in across:
            owner = index(a, b, core)
            arrive(owner)
            send(place(owner), owner, twin)
    for a in [line] + along:
        for b in [square] + across:
            arrive(index(a, b, other))
    for copy in started:
        copy.wait_send()


def wave_table(count, grid, mode):
    phase = 2.0 * math.pi * ((grid * mode) % count) / count
    return np.cos(phase), np.sin(phase)


def interpolate(
    modes,
    orders,
    order_count,
    shard_count,
    coeffs_ref,
    visit_ref,
    phi_table_ref,
    psi_table_ref,
    slot_ref,
    phi_ref,
    psi_ref,
    fraction_ref,
    out_ref,
    picked,
    edge,
    synth,
    wave_a,
    wave_b,
    values_a,
    values_b,
):
    terms = 2 * orders
    high = PHI_T // LOW
    theta = coeffs_ref.shape[1]
    depth, owners = visit_ref.shape
    slots = owners * depth
    blocks = NPHI // (order_count * PHI_T)
    groups = slots // LANES
    listed = jnp.concatenate([visit_ref[d : d + 1, :] for d in range(depth)], axis=1)
    for g in range(groups):
        lanes = slice(g * LANES, (g + 1) * LANES)
        tile = jnp.maximum(listed[:, lanes], 0)
        owner = (lax.broadcasted_iota(jnp.int32, (1, LANES), 1) + g * LANES) % owners
        row = (owner % shard_count) * (theta // shard_count) + tile // blocks
        first_phi = (owner // shard_count) * (NPHI // order_count) + (tile % blocks) * PHI_T
        chosen = (
            lax.broadcasted_iota(jnp.int32, (theta, LANES), 0) == row
        ).astype(jnp.float32).astype(jnp.bfloat16)

        def pick(m, carry):
            rows = pl.ds(pl.multiple_of(m * 4 * terms, 4 * terms), 4 * terms)
            picked[rows, :] = jnp.dot(
                coeffs_ref[rows, :], chosen, preferred_element_type=jnp.float32
            )
            return carry

        lax.fori_loop(0, modes // 4, pick, 0)
        turn = (lax.broadcasted_iota(jnp.int32, (modes, LANES), 0) * first_phi) % NPHI
        angle = turn.astype(jnp.float32) * (2.0 * math.pi / NPHI)
        turn_cos, turn_sin = jnp.cos(angle), jnp.sin(angle)

        def sum_modes(k, carry):
            real = picked[pl.ds(2 * k, modes, stride=terms), :]
            imag = picked[pl.ds(2 * k + 1, modes, stride=terms), :]
            turned = jnp.concatenate(
                [turn_cos * real - turn_sin * imag, turn_sin * real + turn_cos * imag], axis=0
            ).astype(jnp.bfloat16)
            values = jnp.dot(phi_table_ref[...], turned, preferred_element_type=jnp.float32)
            for h in range(high):
                synth[
                    pl.ds(pl.multiple_of(k * 2 * LOW, 2 * LOW), 2 * LOW),
                    h * slots + g * LANES : h * slots + (g + 1) * LANES,
                ] = values[h * 2 * LOW : (h + 1) * 2 * LOW].astype(jnp.bfloat16)
            edge[pl.ds(pl.multiple_of(k * 2 * high, 2 * high), 2 * high), :] = values[
                2 * PHI_T :
            ]
            return carry

        lax.fori_loop(0, orders, sum_modes, 0, unroll=4)
        for part in range(2):
            for h in range(high):
                synth[
                    terms * LOW + part * orders : terms * LOW + (part + 1) * orders,
                    h * slots + g * LANES : h * slots + (g + 1) * LANES,
                ] = edge[pl.ds(part * high + h, orders, stride=2 * high), :].astype(jnp.bfloat16)

    def begin(i, values, wave):
        phi, psi = phi_ref[i], psi_ref[i]
        along_psi = fraction_ref[i][1:2]
        slot = slot_ref[i]
        key = ((phi // LOW) * depth + slot % depth) * owners + slot // depth
        entry = (
            lax.broadcasted_iota(jnp.int32, (high * slots, CHUNK), 0) == key
        ).astype(jnp.float32).astype(jnp.bfloat16)
        at_psi = lax.broadcasted_iota(jnp.int32, (NPSI, CHUNK), 0)
        weight = jnp.where(
            at_psi == psi, 1.0 - along_psi, jnp.where(at_psi == (psi + 1) % NPSI, along_psi, 0.0)
        )
        coarse = weight.astype(jnp.bfloat16)
        fine = (weight - coarse.astype(jnp.float32)).astype(jnp.bfloat16)
        wave[...] = jnp.dot(
            psi_table_ref[...],
            jnp.concatenate([coarse, fine], axis=0),
            preferred_element_type=jnp.float32,
        )
        values[...] = jnp.dot(synth[...], entry, preferred_element_type=jnp.float32)

    def finish(i, values, wave):
        phi = phi_ref[i]
        along_phi = fraction_ref[i][0:1]
        sums = [jnp.zeros((LOW, CHUNK), jnp.float32) for _ in range(4)]
        for k in range(orders):
            for part in range(2):
                at = (2 * k + part) * LOW
                line = part * orders + k
                sums[at // LOW % 4] += values[at : at + LOW, :] * wave[line : line + 1, :]
        inner = (sums[0] + sums[1]) + (sums[2] + sums[3])
        last = jnp.sum(values[terms * LOW :, :] * wave[...], axis=0, keepdims=True)
        low = phi % LOW
        at_low = lax.broadcasted_iota(jnp.int32, (LOW, CHUNK), 0)
        weight_phi = jnp.where(
            at_low == low, 1.0 - along_phi, jnp.where(at_low == low + 1, along_phi, 0.0)
        )
        total = jnp.sum(inner * weight_phi, axis=0, keepdims=True)
        out_ref[i] = total + jnp.where(low == LOW - 1, along_phi, 0.0) * last

    chunks = slot_ref.shape[0]
    begin(0, values_a, wave_a)

    def pair(i, carry):
        begin(2 * i + 1, values_b, wave_b)
        finish(2 * i, values_a, wave_a)
        begin(jnp.minimum(2 * i + 2, chunks - 1), values_a, wave_a)
        finish(2 * i + 1, values_b, wave_b)
        return carry

    lax.fori_loop(0, chunks // 2, pair, 0)


def phi_rows(modes):
    mode = np.arange(modes, dtype=np.int64)[None, :]
    high = PHI_T // LOW
    cos, sin = wave_table(NPHI, np.arange(PHI_T, dtype=np.int64)[:, None], mode)
    real = np.concatenate([cos, -sin], axis=1)
    imag = np.concatenate([sin, cos], axis=1)
    inner = np.stack(
        [real.reshape(high, LOW, 2 * modes), imag.reshape(high, LOW, 2 * modes)], axis=1
    ).reshape(2 * PHI_T, 2 * modes)
    zero = np.zeros((1, 2 * modes), np.float64)
    edge = np.concatenate([real[LOW::LOW], zero, imag[LOW::LOW], zero], axis=0)
    return jnp.asarray(np.concatenate([inner, edge], axis=0), jnp.bfloat16)


def psi_rows(orders):
    order = np.arange(orders, dtype=np.int64)[:, None]
    cos, sin = wave_table(NPSI, np.arange(NPSI, dtype=np.int64)[None, :], order)
    half = np.concatenate([cos, -sin], axis=0)
    return jnp.asarray(np.concatenate([half, half], axis=1), jnp.bfloat16)


def shards(sky_coeffs, beam_coeffs, wigner, visits, point_slot, phi_cell, psi_cell, fraction):
    order_count = lax.axis_size("order")
    shard_count = lax.axis_size("shard")
    local_modes = sky_coeffs.shape[0]
    local_orders = beam_coeffs.shape[0]
    theta_count = wigner.shape[3]
    orders = local_orders * order_count
    modes = local_modes * shard_count
    weighted = (sky_coeffs[:, None, :, :] * beam_coeffs[None, :, None, :]).astype(jnp.bfloat16)
    coeffs = jnp.einsum("mkcl,mklt->mkct", weighted, wigner, preferred_element_type=jnp.float32)
    coeffs = coeffs.astype(jnp.bfloat16).reshape(local_modes * local_orders * 2, theta_count)
    coeffs = pl.pallas_call(
        functools.partial(gather_blocks, shard_count // (SQUARE * CORES)),
        out_shape=jax.ShapeDtypeStruct((shard_count * coeffs.shape[0], theta_count), jnp.bfloat16),
        in_specs=[pl.BlockSpec(memory_space=pltpu.VMEM)],
        out_specs=pl.BlockSpec(memory_space=pltpu.VMEM),
        scratch_shapes=[
            pltpu.SemaphoreType.DMA((shard_count - 1,)),
            pltpu.SemaphoreType.DMA((shard_count,)),
        ],
        compiler_params=pltpu.CompilerParams(collective_id=0, has_side_effects=True),
    )(coeffs)
    if order_count > 1:
        coeffs = coeffs.reshape(modes, local_orders * 2, theta_count)
        coeffs = lax.all_gather(coeffs, "order", axis=1, tiled=True)
        coeffs = coeffs.reshape(modes * orders * 2, theta_count)

    slots = visits.shape[1] * visits.shape[2]
    count = point_slot.shape[0]
    chunks = count // CHUNK
    lined = (chunks, 1, CHUNK)
    pairs = jnp.transpose(fraction.reshape(2, chunks, CHUNK), (1, 0, 2))
    high = PHI_T // LOW
    timeline = pl.pallas_call(
        functools.partial(
            interpolate, modes, orders, order_count, shard_count
        ),
        out_shape=jax.ShapeDtypeStruct(lined, jnp.float32),
        in_specs=[pl.BlockSpec(memory_space=pltpu.VMEM)] * 8,
        out_specs=pl.BlockSpec(memory_space=pltpu.VMEM),
        scratch_shapes=[
            pltpu.VMEM((modes * orders * 2, LANES), jnp.float32),
            pltpu.VMEM((orders * 2 * high, LANES), jnp.float32),
            pltpu.VMEM((orders * 2 * (LOW + 1), high * slots), jnp.bfloat16),
            pltpu.VMEM((orders * 2, CHUNK), jnp.float32),
            pltpu.VMEM((orders * 2, CHUNK), jnp.float32),
            pltpu.VMEM((orders * 2 * (LOW + 1), CHUNK), jnp.float32),
            pltpu.VMEM((orders * 2 * (LOW + 1), CHUNK), jnp.float32),
        ],
    )(
        coeffs,
        jnp.transpose(visits[0]),
        phi_rows(modes),
        psi_rows(orders),
        point_slot.reshape(lined),
        phi_cell.reshape(lined),
        psi_cell.reshape(lined),
        pairs,
    )
    return timeline.reshape(count)


def solution(mesh):
    placed = (
        P("shard", None, None),
        P("order", None),
        P("shard", "order", None, None),
        P(("order", "shard"), None, None),
        P(("order", "shard")),
        P(("order", "shard")),
        P(("order", "shard")),
        P(None, ("order", "shard")),
    )
    return jax.shard_map(
        shards, mesh=mesh, in_specs=placed, out_specs=P(("order", "shard")), check_vma=False
    )
```

profile of v0, /device:TPU:0, one launch (start us, length us, event | category | flops | bytes accessed | tf_op | source)
XLA Modules:
  0.0 68.4 jit_solution(13353121812403843078)
XLA Ops:
  0.0 13.7 %fusion.2 = bf16[64,2,128]{2,1,0:T(2,128)(2,1)} fusion(bf16[1,64,2048,128]{3,2,1,0:T(8,128)(2,1)} %param.12, f32[64,2048]{1,0:T(8,128)} %param.11, f32[2,2048]{1,0:T(2,128)} %bitcast.22), kind=kOutput, calls=%fused_computation.2 | convolution fusion | flops 67649536 | bytes 34127872 | tf_op jit(solution)/shard_map/mkcl,mklt->mkct/dot_general | solution.py:262
  13.7 17.5 %shard_map.100.coeffs_ref = bf16[4096,128]{1,0:T(8,128)(2,1)} custom-call(bf16[128,128]{1,0:T(8,128)(2,1)} %bitcast.17), custom_call_target="tpu_custom_call" | custom-call | tf_op jit(solution)/shard_map/pallas_call | solution.py:264
  31.2 37.2 %shard_map.101 = f32[64,1,256]{2,1,0:T(1,128)} custom-call(bf16[4096,128]{1,0:T(8,128)(2,1)} %shard_map.100.coeffs_ref, s32[4,32]{1,0:T(4,128)} %bitcast.23, bf16[72,64]{1,0:T(8,128)(2,1)} %constant.4.clone.phi_table_ref, bf16[128,256]{1,0:T(8,128)(2,1)} %constant.5.clone.psi_table_ref, s32[64,1,256]{2,1,0:T(1,128)} %bitcast.19, s32[64,1,256]{2,1,0:T(1,128)} %bitcast.20, ...), custom_call_target="tpu_custom_call" | custom-call | tf_op jit(solution)/shard_map/pallas_call | solution.py:286
where the time goes:
time: 68.6 us; the launch traced here: 68.4 us
  Pallas kernels  54.7 us (80%)
  matrix products  13.7 us (20%)
    pallas_call x1, Pallas kernels, shards(): pl.pallas_call(functools.partial(interpolate, modes, orders, order_count,...  37.2 us
    pallas_call x1, Pallas kernels, shards(): pl.pallas_call(functools.partial(gather_blocks, shard_count // (SQUARE *...  17.5 us
    dot_general x1, matrix products, shards(): jnp.einsum('mkcl,mklt->mkct', weighted, wigner, preferred_element_type=jn...  13.7 us

commit v1 on v0

--- a/solution.py
+++ b/solution.py
@@ -15,10 +15,248 @@
 LOW = 8
 LANES = 128
 CHUNK = 256
+KB = 8
+BLOCK = 256
+F32, BF16, I32 = jnp.float32, jnp.bfloat16, jnp.int32
 
 
 SQUARE = 4
 CORES = 2
+
+
+NT = (((1,), (1,)), ((), ()))
+
+
+def hot(index, size):
+    n = index.shape[1]
+    return lax.broadcasted_iota(I32, (size, n), 0) == index
+
+
+def wave(count, grid, mode):
+    phase = 2.0 * math.pi * ((grid * mode) % count) / count
+    return np.cos(phase), np.sin(phase)
+
+
+def phi_matrix(modes):
+    m = np.arange(modes)[None, :]
+    cos, sin = wave(NPHI, np.arange(PHI_T)[:, None], m)
+    eye = np.eye(KB)
+    core = np.stack([np.stack([cos, -sin], -1), np.stack([sin, cos], -1)], 1)
+    full = np.einsum("pamc,kj->pakmcj", core, eye)
+    return jnp.asarray(full.reshape(PHI_T * 2 * KB, modes * 2 * KB), BF16)
+
+
+def psi_matrix(orders):
+    k = np.arange(orders)[None, :]
+    cos, sin = wave(NPSI, np.arange(NPSI)[:, None], k)
+    pair = np.stack([cos.reshape(NPSI, -1, KB), -sin.reshape(NPSI, -1, KB)], 2)
+    return jnp.asarray(pair.reshape(NPSI, 2 * orders), BF16)
+
+
+def rank_matrix():
+    i = np.arange(BLOCK)
+    upper = (i[:, None] < i[None, :]).astype(np.float32)
+    return jnp.asarray(np.concatenate([upper, np.ones((BLOCK, LANES), np.float32)], 1), BF16)
+
+
+def prepare(owners, depth, unit, slot_ref, phi_ref, psi_ref, frac_ref, rank_ref,
+            dest_ref, sorted_ref, chunk_ref, carry, counts, stack, acc):
+    blocks = slot_ref.shape[0]
+    terms = 6
+
+    def own(b):
+        return hot(slot_ref[pl.ds(b, 1), :] // depth, owners)
+
+    def count(b, total):
+        return total + jnp.where(own(b), 1.0, 0.0)
+
+    total = lax.fori_loop(0, blocks, count, jnp.zeros((owners, BLOCK), F32), unroll=4)
+    ones = jnp.ones((BLOCK, LANES), BF16)
+    units = jnp.dot(total.astype(BF16), ones, preferred_element_type=F32) * (1.0 / unit)
+    below = (
+        lax.broadcasted_iota(I32, (owners, owners), 0) > lax.broadcasted_iota(I32, (owners, owners), 1)
+    ).astype(F32).astype(BF16)
+    start = jnp.dot(below, units.astype(BF16), preferred_element_type=F32)
+    lane = lax.broadcasted_iota(I32, (owners, LANES), 1).astype(F32)
+    chunk_ref[...] = jnp.sum(jnp.where(start + units <= lane, 1.0, 0.0), axis=0, keepdims=True).astype(I32)
+    carry[...] = start * unit
+
+    def rank(b, c):
+        mask = own(b)
+        found = jnp.dot(jnp.where(mask, 1.0, 0.0).astype(BF16), rank_ref[...], preferred_element_type=F32)
+        base = carry[...]
+        spot = found[:, :BLOCK] + jnp.concatenate([base] * (BLOCK // LANES), axis=1)
+        dest_ref[pl.ds(b, 1), :] = jnp.sum(jnp.where(mask, spot, 0.0), axis=0, keepdims=True).astype(I32)
+        carry[...] = base + found[:, BLOCK:]
+        return c
+
+    lax.fori_loop(0, blocks, rank, 0, unroll=2)
+    acc[...] = jnp.zeros_like(acc)
+    group = 4
+
+    def move(g, c):
+        rows, lanes = [], []
+        for u in range(group):
+            b = g * group + u
+            dest = dest_ref[pl.ds(b, 1), :]
+            slot = slot_ref[pl.ds(b, 1), :]
+            at = (phi_ref[pl.ds(b, 1), :] * depth + slot % depth).astype(F32)
+            psi = psi_ref[pl.ds(b, 1), :].astype(F32)
+            along, across = frac_ref[0, pl.ds(b, 1), :], frac_ref[1, pl.ds(b, 1), :]
+            along_c, across_c = along.astype(BF16).astype(F32), across.astype(BF16).astype(F32)
+            row = hot(dest // LANES, LANES)
+            parts = [at, psi, along_c, along - along_c, across_c, across - across_c]
+            rows.append(jnp.concatenate([jnp.where(row, p, 0.0).astype(BF16) for p in parts], axis=0))
+            lanes.append(jnp.where(hot(dest % LANES, LANES), 1.0, 0.0).astype(BF16))
+        acc[...] += lax.dot_general(
+            jnp.concatenate(rows, axis=1), jnp.concatenate(lanes, axis=1), NT, preferred_element_type=F32
+        )
+        return c
+
+    lax.fori_loop(0, blocks // group, move, 0)
+    r = LANES
+    sorted_ref[0] = acc[0:r]
+    sorted_ref[1] = acc[r:2 * r]
+    sorted_ref[2] = acc[2 * r:3 * r] + acc[3 * r:4 * r]
+    sorted_ref[3] = acc[4 * r:5 * r] + acc[5 * r:6 * r]
+
+
+def convolve(modes, orders, owners, depth, chunk_ref, coeffs_ref, visit_ref, phi_mat, psi_mat,
+             sorted_ref, dest_ref, out_ref, synth, lines, table, found):
+    slots = owners * depth
+    theta = coeffs_ref.shape[1]
+    blocks = NPHI // PHI_T
+    steps = orders // KB
+    wide = 2 * KB
+    tile = jnp.maximum(jnp.concatenate([visit_ref[d:d + 1, :] for d in range(depth)], axis=1), 0)
+    owner = lax.broadcasted_iota(I32, (1, slots), 1) % owners
+    row = owner * (theta // owners) + tile // blocks
+    first = (tile % blocks) * PHI_T
+    pick = jnp.where(hot(row, theta), 1.0, 0.0).astype(BF16)
+    turn = (lax.broadcasted_iota(I32, (modes, slots), 0) * first) % NPHI
+    angle = turn.astype(F32) * (2.0 * math.pi / NPHI)
+    cos, sin = jnp.cos(angle), jnp.sin(angle)
+
+    def step(j, c):
+        rows = jnp.concatenate(
+            [coeffs_ref[pl.ds(pl.multiple_of(m * 2 * orders + j * wide, wide), wide), :] for m in range(modes)], axis=0
+        )
+        x = jnp.dot(rows, pick, preferred_element_type=F32)
+        turned = []
+        for m in range(modes):
+            re, im = x[m * wide:m * wide + KB], x[m * wide + KB:(m + 1) * wide]
+            cm, sm = cos[m:m + 1], sin[m:m + 1]
+            turned.append(jnp.concatenate([cm * re - sm * im, sm * re + cm * im], axis=0).astype(BF16))
+        y = jnp.dot(phi_mat[...], jnp.concatenate(turned, axis=0), preferred_element_type=F32)
+        for p in range(PHI_T):
+            synth[p, pl.ds(pl.multiple_of(j * wide, wide), wide), :] = y[p * wide:(p + 1) * wide].astype(BF16)
+        return c
+
+    lax.fori_loop(0, steps, step, 0)
+    eye = (
+        lax.broadcasted_iota(I32, (slots, slots), 0) == lax.broadcasted_iota(I32, (slots, slots), 1)
+    ).astype(F32).astype(BF16)
+
+    def flip(p, c):
+        lines[pl.ds(pl.multiple_of(p * slots, slots), slots), :] = lax.dot_general(
+            eye, synth[p], NT, preferred_element_type=F32)
+        return c
+
+    lax.fori_loop(0, PHI_T, flip, 0, unroll=4)
+
+    def cube(o, c):
+        part = lines[pl.ds(o, PHI_T * depth, stride=owners), :].astype(BF16)
+        t = lax.dot_general(psi_mat[...], part, NT, preferred_element_type=F32).astype(BF16)
+        table[pl.ds(pl.multiple_of(o * NPSI, NPSI), NPSI), :] = jnp.concatenate([t, t], axis=1)
+        return c
+
+    lax.fori_loop(0, owners, cube, 0, unroll=4)
+    per = BLOCK // LANES
+
+    def wide_row(i, c):
+        return jnp.concatenate([sorted_ref[i, pl.ds(c * per + u, 1), :] for u in range(per)], axis=1)
+
+    def chunk(c, s):
+        o = chunk_ref[0, c]
+        at, psi = wide_row(0, c).astype(I32), wide_row(1, c).astype(I32)
+        along, across = wide_row(2, c), wide_row(3, c)
+        spots = lax.broadcasted_iota(I32, (PHI_T * depth, BLOCK), 0)
+        w = jnp.where(spots == at, 1.0 - along, jnp.where(spots == at + depth, along, 0.0))
+        coarse = w.astype(BF16)
+        fine = (w - coarse.astype(F32)).astype(BF16)
+        t = table[pl.ds(pl.multiple_of(o * NPSI, NPSI), NPSI), :]
+        g = jnp.dot(t, jnp.concatenate([coarse, fine], axis=0), preferred_element_type=F32)
+        angles = lax.broadcasted_iota(I32, (NPSI, BLOCK), 0)
+        v = jnp.where(angles == psi, 1.0 - across, jnp.where(angles == (psi + 1) % NPSI, across, 0.0))
+        line = jnp.sum(g * v, axis=0, keepdims=True)
+        for u in range(per):
+            found[pl.ds(c * per + u, 1), :] = line[:, u * LANES:(u + 1) * LANES]
+        return s
+
+    count = dest_ref.shape[0]
+    lax.fori_loop(0, count, chunk, 0, unroll=2)
+    values = found[...]
+    coarse = values.astype(BF16)
+    fine = (values - coarse.astype(F32)).astype(BF16)
+    both = jnp.concatenate([coarse, fine], axis=1)
+
+    def back(b, s):
+        dest = dest_ref[pl.ds(b, 1), :]
+        lanes = jnp.where(hot(dest % LANES, LANES), 1.0, 0.0).astype(BF16)
+        h = jnp.dot(both, jnp.concatenate([lanes, lanes], axis=0), preferred_element_type=F32)
+        out_ref[pl.ds(b, 1), :] = jnp.sum(jnp.where(hot(dest // LANES, LANES), h, 0.0), axis=0, keepdims=True)
+        return s
+
+    lax.fori_loop(0, count, back, 0, unroll=2)
+
+
+V = pl.BlockSpec(memory_space=pltpu.VMEM)
+
+
+def run_prepare(point_slot, phi_cell, psi_cell, fraction, owners, depth):
+    count = point_slot.shape[0]
+    blocks = count // BLOCK
+    unit = count // owners // 2
+    return pl.pallas_call(
+        functools.partial(prepare, owners, depth, unit),
+        out_shape=(
+            jax.ShapeDtypeStruct((blocks, BLOCK), I32),
+            jax.ShapeDtypeStruct((4, LANES, LANES), F32),
+            jax.ShapeDtypeStruct((1, LANES), I32),
+        ),
+        in_specs=[V] * 5,
+        out_specs=(V, V, V),
+        scratch_shapes=[
+            pltpu.VMEM((owners, LANES), F32),
+            pltpu.VMEM((owners, LANES), F32),
+            pltpu.VMEM((8, LANES), F32),
+            pltpu.VMEM((6 * LANES, LANES), F32),
+        ],
+        name="prepare",
+    )(point_slot.reshape(blocks, BLOCK), phi_cell.reshape(blocks, BLOCK), psi_cell.reshape(blocks, BLOCK),
+      fraction.reshape(2, blocks, BLOCK), rank_matrix())
+
+
+def run_convolve(coeffs, visits, dest, spots, chunks, modes, orders):
+    owners, depth = visits.shape
+    slots = owners * depth
+    return pl.pallas_call(
+        functools.partial(convolve, modes, orders, owners, depth),
+        out_shape=jax.ShapeDtypeStruct(dest.shape, F32),
+        in_specs=[pl.BlockSpec(memory_space=pltpu.SMEM)] + [V] * 6,
+        out_specs=V,
+        scratch_shapes=[
+            pltpu.VMEM((PHI_T, 2 * orders, slots), BF16),
+            pltpu.VMEM((PHI_T * slots, 2 * orders), F32),
+            pltpu.VMEM((owners * NPSI, 2 * LANES), BF16),
+            pltpu.VMEM((LANES, LANES), F32),
+        ],
+        name="convolve",
+    )(chunks, coeffs, jnp.transpose(visits), phi_matrix(modes), psi_matrix(orders), spots, dest)
+
+def grouped(order_count, visits, count):
+    owners, depth = visits[1:]
+    return order_count == 1 and owners * depth == LANES and count == LANES * LANES and count % (2 * owners * BLOCK) == 0
 
 
 def gather_blocks(lines, block_ref, out_ref, send_sem, recv_sem):
@@ -260,7 +498,10 @@
     modes = local_modes * shard_count
     weighted = (sky_coeffs[:, None, :, :] * beam_coeffs[None, :, None, :]).astype(jnp.bfloat16)
     coeffs = jnp.einsum("mkcl,mklt->mkct", weighted, wigner, preferred_element_type=jnp.float32)
-    coeffs = coeffs.astype(jnp.bfloat16).reshape(local_modes * local_orders * 2, theta_count)
+    coeffs = coeffs.astype(jnp.bfloat16)
+    if grouped(order_count, visits.shape, point_slot.shape[0]):
+        coeffs = coeffs.reshape(local_modes, orders // KB, KB, 2, theta_count).transpose(0, 1, 3, 2, 4)
+    coeffs = coeffs.reshape(local_modes * local_orders * 2, theta_count)
     coeffs = pl.pallas_call(
         functools.partial(gather_blocks, shard_count // (SQUARE * CORES)),
         out_shape=jax.ShapeDtypeStruct((shard_count * coeffs.shape[0], theta_count), jnp.bfloat16),
@@ -279,6 +520,11 @@
 
     slots = visits.shape[1] * visits.shape[2]
     count = point_slot.shape[0]
+    owners, depth = visits.shape[1:]
+    unit = count // (2 * owners)
+    if grouped(order_count, visits.shape, count):
+        dest, spots, chunks = run_prepare(point_slot, phi_cell, psi_cell, fraction, owners, depth)
+        return run_convolve(coeffs, visits[0], dest, spots, chunks, modes, orders).reshape(count)
     chunks = count // CHUNK
     lined = (chunks, 1, CHUNK)
     pairs = jnp.transpose(fraction.reshape(2, chunks, CHUNK), (1, 0, 2))

time: 68.6 us -> 78.8 us (1.15)
  Pallas kernels: 54.7 us -> 60.6 us
  local copies, waits for them, and re-layouts: 0 us -> 4.74 us
    pallas_call x1 -> x2, Pallas kernels: 37.2 us -> 43.1 us  [the longest x1 25.1 us: run_convolve(): pl.pallas_call(functools.partial(convolve, modes, orders, owners, depth),...]
    reshape x0 -> x4, local copies, waits for them, and re-layouts: none -> 2.56 us  [the longest x1 0.65 us: run_prepare(): phi_cell.reshape(blocks, BLOCK)]
    unnamed x0 -> x10, local copies, waits for them, and re-layouts: none -> 2.18 us
where the time goes in v1:
time: 78.8 us; the launch traced here: 78.5 us
  Pallas kernels  60.6 us (77%)
  matrix products  13.1 us (17%)
  local copies, waits for them, and re-layouts  4.74 us (6%)
    pallas_call x1, Pallas kernels, run_convolve(): pl.pallas_call(functools.partial(convolve, modes, orders, owners, depth),...  25.1 us
    pallas_call x1, Pallas kernels, run_prepare(): pl.pallas_call(functools.partial(prepare, owners, depth, unit), out_shape...  18 us
    pallas_call x1, Pallas kernels, shards(): pl.pallas_call(functools.partial(gather_blocks, shard_count // (SQUARE *...  17.5 us
    dot_general x1, matrix products, shards(): jnp.einsum('mkcl,mklt->mkct', weighted, wigner, preferred_element_type=jn...  13.1 us
    unnamed x10, local copies, waits for them, and re-layouts  2.18 us

profile of v1, /device:TPU:0, one launch (start us, length us, event | category | flops | bytes accessed | tf_op | source)
XLA Modules:
  0.0 78.5 jit_solution(8912506803962645705)
XLA Ops:
  0.0 0.0 copy-start
  0.0 0.0 copy-start.3
  0.0 0.0 copy-start.2
  0.0 0.0 copy-start.1
  0.0 13.1 %fusion.2 = bf16[64,2,128]{2,1,0:T(2,128)(2,1)S(1)} fusion(bf16[1,64,2048,128]{3,2,1,0:T(8,128)(2,1)} %param.13, f32[64,2048]{1,0:T(8,128)} %param.12, f32[2,2048]{1,0:T(2,128)} %bitcast.24), kind=kOutput, calls=%fused_computation.2 | convolution fusion | flops 67649536 | bytes 34127872 | tf_op jit(solution)/shard_map/mkcl,mklt->mkct/dot_general | solution.py:500
  13.1 0.6 copy.12
  13.7 0.0 copy-done.1
  13.7 0.6 reshape.36.slot_ref
  14.4 0.0 copy-done.2
  14.4 0.7 reshape.37.phi_ref
  15.0 0.0 copy-done.3
  15.0 0.6 reshape.38.psi_ref
  15.7 0.0 copy-done
  15.7 0.7 copy.16
  16.4 18.0 %prepare.1 = (s32[64,256]{1,0:T(8,128)}, f32[4,128,128]{2,1,0:T(8,128)}, s32[1,128]{1,0:T(1,128)}) custom-call(s32[64,256]{1,0:T(8,128)} %reshape.36.slot_ref, s32[64,256]{1,0:T(8,128)} %reshape.37.phi_ref, s32[64,256]{1,0:T(8,128)} %reshape.38.psi_ref, f32[2,64,256]{2,1,0:T(8,128)} %bitcast.19, bf16[256,384]{1,0:T(8,128)(2,1)} %constant.6.clone.rank_ref), custom_call_target="tpu_custom_call" | custom-call | tf_op jit(solution)/shard_map/prepare/pallas_call | solution.py:220
  34.4 17.5 %shard_map.109.coeffs_ref = bf16[4096,128]{1,0:T(8,128)(2,1)} custom-call(bf16[128,128]{1,0:T(8,128)(2,1)} %bitcast.22), custom_call_target="tpu_custom_call" | custom-call | tf_op jit(solution)/shard_map/pallas_call | solution.py:505
  51.9 25.1 %convolve.1 = f32[64,256]{1,0:T(8,128)} custom-call(s32[1,128]{1,0:T(1,128)} %get-tuple-element.8.chunk_ref, bf16[4096,128]{1,0:T(8,128)(2,1)} %shard_map.109.coeffs_ref, s32[4,32]{1,0:T(4,128)} %bitcast.25, bf16[512,512]{1,0:T(8,128)(2,1)} %constant.7.clone.phi_mat, bf16[128,128]{1,0:T(8,128)(2,1)} %constant.8.clone.psi_mat, ...), custom_call_target="tpu_custom_call" | custom-call | tf_op jit(solution)/shard_map/convolve/pallas_call | solution.py:243
  77.0 1.5 %copy.14 = f32[8,2,8,128]{3,1,2,0:T(2,128)} copy(f32[8,2,8,128]{3,2,1,0:T(8,128)} %bitcast.20) | data formatting | bytes 131072
Async XLA Ops:
  0.0 15.7 %copy-start = (f32[2,16384]{1,0:T(2,128)S(1)}, f32[2,16384]{1,0:T(2,128)}, u32[]{:S(2)}) copy-start(f32[2,16384]{1,0:T(2,128)} %param.18) | copy-start | bytes 393220
  0.0 15.0 %copy-start.3 = (s32[16384]{0:T(1024)S(1)}, s32[16384]{0:T(1024)}, u32[]{:S(2)}) copy-start(s32[16384]{0:T(1024)} %param.17) | copy-start | bytes 196612
  0.0 14.4 %copy-start.2 = (s32[16384]{0:T(1024)S(1)}, s32[16384]{0:T(1024)}, u32[]{:S(2)}) copy-start(s32[16384]{0:T(1024)} %param.16) | copy-start | bytes 196612
  0.0 13.7 %copy-start.1 = (s32[16384]{0:T(1024)S(1)}, s32[16384]{0:T(1024)}, u32[]{:S(2)}) copy-start(s32[16384]{0:T(1024)} %param.15) | copy-start | bytes 196612
